TPU v7x, 128 devices: a whole 4x4x4 slice. The times are simulated.
128 devices in a mesh: seg: 4 (over z_lo, core), batch: 32 (over z_hi, y, x).
Axes of the slice: x: 4, y: 4, z: 4 (z_hi: 2, z_lo: 2; z = z_hi * 2 + z_lo), core: 2. Of those that a mesh axis runs over, the one named last changes fastest.
Arguments:
- starts: float32 [4, 4096, 1024], P('seg', 'batch'), may hold values from -6 to 6
- targets: float32 [4, 4096, 1024], P('seg', 'batch'), may hold values from -6 to 6
- counts: int32 [4], P('seg'), may hold values from 1 to 3, as said below
- w_in: bfloat16 [1024, 1024], P('batch'), may hold values from -0.1875 to 0.1875
- b_in: float32 [1024], replicated, may hold values from -3 to 3
- w_out: bfloat16 [1024, 1024], P('batch'), may hold values from -0.1875 to 0.1875
Outputs:
- grad_starts: float32 [4, 4096, 1024], P('seg', 'batch')
- grad_w_in: float32 [1024, 1024], P('batch')
- grad_w_out: float32 [1024, 1024], P('batch')
- grad_b_in: float32 [1024], P('batch')
Inputs may be any that keep to these rules, and one draw needn't show every extreme that they name: `counts`: some segment takes 3 steps and some takes 1.
All inputs are finite; a program needn't handle non-finite values.
Results may differ from a plain program's by a relative error of at most 0.00125.
Values may be sent and summed in bfloat16 or wider, within the bound.
No kernel may reach another device: no remote copies, remote signals or barrier semaphores. Data moves between devices by JAX's collectives and lax.ppermute only.
A program may use at most 64 MiB of HBM per device.

v0:
```python
import math
import jax
import jax.numpy as jnp
from jax import lax
from jax.sharding import PartitionSpec as P

D = 1024
MAXSTEP = 3
time_step = 0.25
penalty = 1.0


def shifted(block, axis, distance):
    devices = range(lax.axis_size(axis))
    route = [(i - distance, i) for i in devices if i - distance in devices]
    return lax.ppermute(block, axis, route)


def contract_rows(left, right):
    return lax.dot_general(
        left, right, (((0,), (0,)), ((), ())), preferred_element_type=jnp.float32
    )


def contract_cols(left, right):
    return lax.dot_general(
        left, right, (((1,), (1,)), ((), ())), preferred_element_type=jnp.float32
    )


def vector_field(current, w_in, b_in, w_out):
    inputs = current.astype(jnp.bfloat16)
    hidden = jnp.tanh(jnp.dot(inputs, w_in, preferred_element_type=jnp.float32) + b_in)
    slope = jnp.dot(hidden.astype(jnp.bfloat16), w_out, preferred_element_type=jnp.float32)
    return (slope, inputs, hidden)


def runge_kutta(current, w_in, b_in, w_out):
    slope_one, in_one, hid_one = vector_field(current, w_in, b_in, w_out)
    slope_two, in_two, hid_two = vector_field(
        current + 0.5 * time_step * slope_one, w_in, b_in, w_out
    )
    slope_three, in_three, hid_three = vector_field(
        current + 0.5 * time_step * slope_two, w_in, b_in, w_out
    )
    slope_four, in_four, hid_four = vector_field(
        current + time_step * slope_three, w_in, b_in, w_out
    )
    updated = current + time_step / 6.0 * (
        slope_one + 2.0 * slope_two + 2.0 * slope_three + slope_four
    )
    inputs = jnp.stack([in_one, in_two, in_three, in_four])
    hiddens = jnp.stack([hid_one, hid_two, hid_three, hid_four])
    return (updated, inputs, hiddens)


def field_back(hidden, outer, w_in, w_out):
    outer_low = outer.astype(jnp.bfloat16)
    inner = contract_cols(outer_low, w_out) * (1.0 - hidden * hidden)
    inner_low = inner.astype(jnp.bfloat16)
    return (contract_cols(inner_low, w_in), outer_low, inner_low, jnp.sum(inner, axis=0))


def runge_kutta_back(state_bar, inputs, hiddens, w_in, w_out):
    back_four, outer_four, inner_four, bias_four = field_back(
        hiddens[3], time_step / 6.0 * state_bar, w_in, w_out
    )
    back_three, outer_three, inner_three, bias_three = field_back(
        hiddens[2], time_step / 3.0 * state_bar + time_step * back_four, w_in, w_out
    )
    back_two, outer_two, inner_two, bias_two = field_back(
        hiddens[1], time_step / 3.0 * state_bar + 0.5 * time_step * back_three, w_in, w_out
    )
    back_one, outer_one, inner_one, bias_one = field_back(
        hiddens[0], time_step / 6.0 * state_bar + 0.5 * time_step * back_two, w_in, w_out
    )
    new_bar = state_bar + back_one + back_two + back_three + back_four
    outers = jnp.concatenate([outer_one, outer_two, outer_three, outer_four], axis=0)
    inners = jnp.concatenate([inner_one, inner_two, inner_three, inner_four], axis=0)
    flat_inputs = inputs.reshape(-1, inputs.shape[-1])
    flat_hidden = hiddens.astype(jnp.bfloat16).reshape(-1, hiddens.shape[-1])
    grad_in_step = contract_rows(flat_inputs, inners)
    grad_out_step = contract_rows(flat_hidden, outers)
    grad_bias_step = bias_one + bias_two + bias_three + bias_four
    return (new_bar, grad_in_step, grad_out_step, grad_bias_step)


def body(starts, targets, counts, w_in, b_in, w_out):
    full_in, full_out = (
        lax.all_gather(w_in, "batch", axis=0, tiled=True),
        lax.all_gather(w_out, "batch", axis=0, tiled=True),
    )
    start_now = starts[0]
    target_now = targets[0]
    step_total = counts[0]
    seg_place = lax.axis_index("seg")
    batch_count = lax.axis_size("batch")
    row_count = start_now.shape[0]

    def advance_plain(step_index, carry):
        current, saved = carry
        saved = lax.dynamic_update_index_in_dim(saved, current, step_index, 0)
        updated, inputs, hiddens = runge_kutta(current, full_in, b_in, full_out)
        return (updated, saved)

    saved_empty = jnp.zeros((MAXSTEP, row_count, D), jnp.float32)
    end_state, saved = lax.fori_loop(0, step_total, advance_plain, (start_now, saved_empty))

    def recall(step_index):
        current = lax.dynamic_index_in_dim(saved, step_index, 0, keepdims=False)
        updated, inputs, hiddens = runge_kutta(current, full_in, b_in, full_out)
        return (inputs, hiddens)

    miss = end_state - target_now
    previous = shifted(end_state, "seg", 1)
    has_prev = (seg_place > 0).astype(jnp.float32)
    gap_here = (previous - start_now) * has_prev
    returned = shifted(penalty * gap_here, "seg", -1)
    end_bar = miss + returned

    def retreat(turn, carry):
        state_bar, acc_in, acc_out, acc_bias = carry
        step_index = step_total - 1 - turn
        inputs, hiddens = recall(step_index)
        new_bar, grad_in_step, grad_out_step, grad_bias_step = runge_kutta_back(
            state_bar, inputs, hiddens, full_in, full_out
        )
        return (new_bar, acc_in + grad_in_step, acc_out + grad_out_step, acc_bias + grad_bias_step)

    initial = (
        end_bar,
        jnp.zeros(full_in.shape, jnp.float32),
        jnp.zeros(full_out.shape, jnp.float32),
        jnp.zeros(b_in.shape, jnp.float32),
    )
    start_bar, total_in, total_out, total_bias = lax.fori_loop(0, step_total, retreat, initial)
    start_term = -(penalty * gap_here)
    grad_starts = (start_bar + start_term)[None]
    scale = 1.0 / math.sqrt(row_count * batch_count)
    scaled_in = total_in * scale
    scaled_out = total_out * scale
    scaled_bias = total_bias * scale
    shares = (
        lax.psum_scatter(scaled_in, "batch", scatter_dimension=0, tiled=True),
        lax.psum_scatter(scaled_out, "batch", scatter_dimension=0, tiled=True),
        lax.psum_scatter(scaled_bias, "batch", scatter_dimension=0, tiled=True),
    )
    grad_in, grad_out, grad_bias = lax.psum((shares[0], shares[1], shares[2]), "seg")
    return (grad_starts, grad_in, grad_out, grad_bias)


def solution(mesh):
    return jax.shard_map(
        body,
        mesh=mesh,
        in_specs=(
            P("seg", "batch", None),
            P("seg", "batch", None),
            P("seg"),
            P("batch", None),
            P(),
            P("batch", None),
        ),
        out_specs=(P("seg", "batch", None), P("batch", None), P("batch", None), P("batch")),
        check_vma=False,
    )
```

profile of v0, /device:TPU:1, one launch (start us, length us, event | category | flops | bytes accessed | tf_op | source)
XLA Modules:
  0.0 728.3 jit_solution(12884548266842338025)
XLA Ops:
  8.7 1.9 copy.12
  10.6 73.6 %all-gather.3.cloned.1.call-done = bf16[1024,1024]{1,0:T(8,128)(2,1)} async-done(((bf16[32,1024]{1,0:T(8,128)(2,1)}), bf16[1024,1024]{1,0:T(8,128)(2,1)}) %all-gather.3.cloned.1.call-update) | async-done | bytes 2097168 | tf_op jit(solution)/shard_map/all_gather | solution.py:90
  84.2 71.7 %all-gather.5.cloned.1.call-done = bf16[1024,1024]{1,0:T(8,128)(2,1)} async-done(((bf16[32,1024]{1,0:T(8,128)(2,1)}), bf16[1024,1024]{1,0:T(8,128)(2,1)}) %all-gather.5.cloned.1.call-update) | async-done | bytes 2097168 | tf_op jit(solution)/shard_map/all_gather | solution.py:91
  157.2 16.5 %while.30 = (s32[]{:T(128)}, f32[128,1024]{1,0:T(8,128)}, f32[3,128,1024]{2,1,0:T(8,128)}, s32[]{:T(128)}, bf16[1024,1024]{1,0:T(8,128)(2,1)}, /*index=5*/f32[10...) while((s32[]{:T(128)}, f32[128,1024]{1,0:T(8,128)}, f32[3,128,1024]{2,1,0:T(8,128)}, ...), condition=%wide.region_1.2_spmd, body=%wide.region_0.1_spmd.sunk | while | flops 2150760448 | bytes 34095276 | solution.py:107
  158.9 3.1 fusion.174
  162.1 3.2 fusion.175
  165.2 3.3 fusion.176
  169.4 3.6 fusion.177
  173.7 36.4 %collective-permute-start = (f32[128,1024]{1,0:T(8,128)}, f32[128,1024]{1,0:T(8,128)S(1)}, u32[]{:S(2)}, u32[]{:S(2)}) collective-permute-start(f32[128,1024]{1,0:T(8,128)} %get-tuple-element.170), channel_id=1, source_target_pairs={{0,32},{32,64},{64,96},{1,33},{33,65},{65,97},{2,34},{34,66},{66,9... | collective-permute-start | bytes 1572872 | tf_op jit(solution)/shard_map/ppermute | solution.py:16
  210.2 6.4 collective-permute-done
  217.7 1.9 collective-permute-start.1
  220.3 8.6 %collective-permute-done.1 = f32[128,1024]{1,0:T(8,128)S(1)} collective-permute-done((f32[128,1024]{1,0:T(8,128)S(1)}, f32[128,1024]{1,0:T(8,128)S(1)}, u32[]{:S(2)}, u32[]{:S(2)}) %collective-permute-start.1) | collective-permute-done | bytes 524320 | tf_op jit(solution)/shard_map/ppermute | solution.py:16
  230.1 2.5 broadcast.45.clone
  232.6 2.5 broadcast.45
  235.1 21.9 %while.31 = (s32[]{:T(128)}, f32[128,1024]{1,0:T(8,128)S(1)}, f32[1024,1024]{1,0:T(8,128)}, f32[1024,1024]{1,0:T(8,128)}, f32[1024]{0:T(1024)S(1)}, /*index=5*/s...) while((s32[]{:T(128)}, f32[128,1024]{1,0:T(8,128)S(1)}, ...), condition=%wide.region_7.8_spmd, body=%wide.region_2.7_spmd.sunk | while | flops 6195249152 | bytes 161800576 | solution.py:136
  254.4 2.0 copy-done.4
  257.1 5.0 broadcast_multiply_fusion.1
  262.1 5.0 broadcast_multiply_fusion
  269.0 80.0 %all-reduce = f32[1024]{0:T(1024)S(1)} all-reduce(f32[1024]{0:T(1024)S(1)} %broadcast_multiply_fusion.2), channel_id=4, replica_groups=mesh['seg'=4,'batch'=32] {'batch'}, use_global_device_ids=true, to_apply=%region_12.13.clone | all-reduce | flops 1024 | bytes 8192
  349.1 58.6 %psum.23 = f32[32]{0:T(128)} all-reduce(f32[32]{0:T(128)S(1)} %dynamic-slice.1), channel_id=1, replica_groups=mesh['seg'=4,'batch'=32] {'seg'}, use_global_device_ids=true, to_apply=%region_13.14 | all-reduce | flops 32 | bytes 256 | tf_op jit(solution)/shard_map/psum | solution.py:148
  407.7 63.2 %reduce-scatter.3.cloned.1.call-done = f32[32,1024]{1,0:T(8,128)} async-done(((f32[1024,1024]{1,0:T(8,128)}), f32[32,1024]{1,0:T(8,128)}) %reduce-scatter.3.cloned.1.call-update) | async-done | bytes 131088 | tf_op jit(solution)/shard_map/reduce_scatter | solution.py:144
  470.9 190.8 %reduce-scatter.5.cloned.1.call-done = f32[32,1024]{1,0:T(8,128)} async-done(((f32[1024,1024]{1,0:T(8,128)}), f32[32,1024]{1,0:T(8,128)}) %reduce-scatter.5.cloned.1.call-update) | async-done | bytes 131088 | tf_op jit(solution)/shard_map/reduce_scatter | solution.py:145
  662.6 56.0 %all-reduce.4.cloned.1.call-done = (f32[32,1024]{1,0:T(8,128)}, f32[32,1024]{1,0:T(8,128)}) async-done(((f32[32,1024]{1,0:T(8,128)}, f32[32,1024]{1,0:T(8,128)}), (f32[32,1024]{1,0:T(8,128)}, f32[32,1024]{1,0:T(8,128)})) %all-reduce.4.cloned.1.call-update) | async-done | bytes 262160 | tf_op jit(solution)/shard_map/psum | solution.py:148
  718.6 1.6 copy.40
  (64 shorter events, 29.2 us)
Async XLA Ops:
  7.2 150.0 %copy-start.8 = (f32[1024]{0:T(1024)S(1)}, f32[1024]{0:T(1024)}, u32[]{:S(2)}) copy-start(f32[1024]{0:T(1024)} %param.14) | copy-start | bytes 12292
  7.2 77.0 %all-gather.3.cloned.1.call-start = ((), (), s32[]{:S(2)}) async-start(), calls=%async_computation.2 | async-start | bytes 2162688 | tf_op jit(solution)/shard_map/all_gather | solution.py:90
  7.9 147.9 %all-gather.5.cloned.1.call-start = ((), (), s32[]{:S(2)}) async-start(), calls=%async_computation.3 | async-start | bytes 2162688 | tf_op jit(solution)/shard_map/all_gather | solution.py:91
  8.7 462.2 %reduce-scatter.3.cloned.1.call-start = ((), (), s32[]{:S(2)}) async-start(), calls=%async_computation.4 | async-start | bytes 4325376 | tf_op jit(solution)/shard_map/reduce_scatter | solution.py:144
  158.9 3.1 copy-start
  173.7 42.9 %collective-permute-start = (f32[128,1024]{1,0:T(8,128)}, f32[128,1024]{1,0:T(8,128)S(1)}, u32[]{:S(2)}, u32[]{:S(2)}) collective-permute-start(f32[128,1024]{1,0:T(8,128)} %get-tuple-element.170), channel_id=1, source_target_pairs={{0,32},{32,64},{64,96},{1,33},{33,65},{65,97},{2,34},{34,66},{66,9... | collective-permute-start | bytes 1572872 | tf_op jit(solution)/shard_map/ppermute | solution.py:16
  217.7 11.1 %collective-permute-start.1 = (f32[128,1024]{1,0:T(8,128)S(1)}, f32[128,1024]{1,0:T(8,128)S(1)}, u32[]{:S(2)}, u32[]{:S(2)}) collective-permute-start(f32[128,1024]{1,0:T(8,128)S(1)} %subtract_multiply_fusion), channel_id=1, source_target_pairs={{32,0},{64,32},{96,64},{33,1},{65,33},{97,65},{34,2},{66,34},{98,6... | collective-permute-start | bytes 1572872 | tf_op jit(solution)/shard_map/ppermute | solution.py:16
  232.6 2.5 copy-start.1
  236.0 2.8 copy-start.2
  236.0 2.8 copy-start.7
  248.1 2.2 copy-start.5
  250.3 2.2 copy-start.3
  252.5 2.0 copy-start.6
  254.4 2.0 copy-start.4
  262.1 399.6 %reduce-scatter.5.cloned.1.call-start = ((), (), s32[]{:S(2)}) async-start(), calls=%async_computation.5 | async-start | bytes 4325376 | tf_op jit(solution)/shard_map/reduce_scatter | solution.py:145
  267.1 0.7 copy-start.9
  267.1 451.5 %all-reduce.4.cloned.1.call-start = ((), (), s32[]{:S(2)}) async-start(), calls=%async_computation.6 | async-start | bytes 524288 | tf_op jit(solution)/shard_map/psum | solution.py:148
Sparse Core Ops, SparseCore 0:
  11.1 73.0 all-gather.2
  87.3 68.5 all-gather.4
  262.2 208.6 reduce-scatter.2
  473.1 188.5 reduce-scatter.4
  664.1 54.4 all-reduce.3
where the time goes:
time: 729 us; the launch traced here: 728 us
  waiting for transfers between devices  472 us (65%)
  blocking collectives  139 us (19%)
  starting transfers between devices  38.6 us (5%)
  matrix products  27.3 us (4%)
  local copies, waits for them, and re-layouts  20.2 us (3%)
  between operations  15.2 us (2%)
  other arithmetic  13.7 us (2%)
    reduce_scatter x1, waiting for transfers between devices, body(): lax.psum_scatter(scaled_out, 'batch', scatter_dimension=0, tiled=True)  191 us
    unnamed x1, blocking collectives  80 us
    all_gather x1, waiting for transfers between devices, body(): lax.all_gather(w_in, 'batch', axis=0, tiled=True)  73.6 us
    all_gather x1, waiting for transfers between devices, body(): lax.all_gather(w_out, 'batch', axis=0, tiled=True)  71.7 us
    reduce_scatter x1, waiting for transfers between devices, body(): lax.psum_scatter(scaled_in, 'batch', scatter_dimension=0, tiled=True)  63.2 us
    psum x1, blocking collectives, body(): lax.psum((shares[0], shares[1], shares[2]), 'seg')  58.6 us
    psum x1, waiting for transfers between devices, body(): lax.psum((shares[0], shares[1], shares[2]), 'seg')  56 us
    ppermute x2, starting transfers between devices, shifted(): return lax.ppermute(block, axis, route)  38.4 us
  transfers between devices with their start and end apart: 7, of which 7 were waited for; matrix products, arithmetic and copies ran while one was open for 1% of the time, Pallas kernels for 0%

commit v1 on v0

--- a/solution.py
+++ b/solution.py
@@ -8,6 +8,13 @@
 MAXSTEP = 3
 time_step = 0.25
 penalty = 1.0
+
+
+def all_by_exchange(value, axis, dim):
+    size = lax.axis_size(axis)
+    blocks = jnp.stack([value for _ in range(size)])
+    blocks = lax.all_to_all(blocks, axis, split_axis=0, concat_axis=0)
+    return jnp.concatenate(blocks, axis=dim)
 
 
 def shifted(block, axis, distance):
@@ -87,7 +94,7 @@
 
 def body(starts, targets, counts, w_in, b_in, w_out):
     full_in, full_out = (
-        lax.all_gather(w_in, "batch", axis=0, tiled=True),
+        all_by_exchange(w_in, "batch", 0),
         lax.all_gather(w_out, "batch", axis=0, tiled=True),
     )
     start_now = starts[0]

time: 729 us -> 673 us (0.923)
  waiting for transfers between devices: 472 us -> 405 us
  starting transfers between devices: 38.6 us -> 48.3 us
    all_gather x1 -> x0, waiting for transfers between devices: 73.6 us -> none  [body(): lax.all_gather(w_in, 'batch', axis=0, tiled=True)]
    all_to_all x0 -> x1, waiting for transfers between devices: none -> 28.3 us  [all_by_exchange(): blocks = lax.all_to_all(blocks, axis, split_axis=0, concat_axis=0)]
    all_gather x1, waiting for transfers between devices: 71.7 us -> 50.2 us  [body(): lax.all_gather(w_out, 'batch', axis=0, tiled=True)]
    all_to_all x0 -> x1, starting transfers between devices: none -> 11.3 us  [all_by_exchange(): blocks = lax.all_to_all(blocks, axis, split_axis=0, concat_axis=0)]
where the time goes in v1:
time: 673 us; the launch traced here: 671 us
  waiting for transfers between devices  405 us (60%)
  blocking collectives  138 us (21%)
  starting transfers between devices  48.3 us (7%)
  matrix products  26.6 us (4%)
  local copies, waits for them, and re-layouts  21.5 us (3%)
  between operations  15.2 us (2%)
  other arithmetic  13.9 us (2%)
    reduce_scatter x1, waiting for transfers between devices, body(): lax.psum_scatter(scaled_out, 'batch', scatter_dimension=0, tiled=True)  192 us
    unnamed x1, blocking collectives  80.2 us
    reduce_scatter x1, waiting for transfers between devices, body(): lax.psum_scatter(scaled_in, 'batch', scatter_dimension=0, tiled=True)  62.5 us
    psum x1, blocking collectives, body(): lax.psum((shares[0], shares[1], shares[2]), 'seg')  58.2 us
    psum x1, waiting for transfers between devices, body(): lax.psum((shares[0], shares[1], shares[2]), 'seg')  56.1 us
    all_gather x1, waiting for transfers between devices, body(): lax.all_gather(w_out, 'batch', axis=0, tiled=True)  50.2 us
    ppermute x2, starting transfers between devices, shifted(): return lax.ppermute(block, axis, route)  36.8 us
    all_to_all x1, waiting for transfers between devices, all_by_exchange(): blocks = lax.all_to_all(blocks, axis, split_axis=0, concat_axis=0)  28.3 us
  transfers between devices with their start and end apart: 7, of which 7 were waited for; matrix products, arithmetic and copies ran while one was open for 1% of the time, Pallas kernels for 0%

profile of v1, /device:TPU:1, one launch (start us, length us, event | category | flops | bytes accessed | tf_op | source)
XLA Modules:
  0.0 671.3 jit_solution(4530539794999310874)
XLA Ops:
  7.9 2.4 stack.86
  10.3 11.3 %all-to-all-start = ((bf16[32,32,1024]{2,1,0:T(8,128)(2,1)}), bf16[32,32,1024]{2,1,0:T(8,128)(2,1)S(1)}, u32[]{:S(2)}, u32[]{:S(2)}) async-start(bf16[32,32,1024]{2,1,0:T(8,128)(2,1)} %stack.86), calls=%async_computation | async-start | bytes 4194304 | tf_op jit(solution)/shard_map/all_to_all | solution.py:16
  22.5 28.3 %all-to-all-done = bf16[32,32,1024]{2,1,0:T(8,128)(2,1)S(1)} async-done(((bf16[32,32,1024]{2,1,0:T(8,128)(2,1)}), bf16[32,32,1024]{2,1,0:T(8,128)(2,1)S(1)}, u32[]{:S(2)}, u32[]{:S(2)}) %all-to-all-start) | async-done | bytes 2097184 | tf_op jit(solution)/shard_map/all_to_all | solution.py:16
  50.8 50.2 %all-gather.2.cloned.1.call-done = bf16[1024,1024]{1,0:T(8,128)(2,1)} async-done(((bf16[32,1024]{1,0:T(8,128)(2,1)}), bf16[1024,1024]{1,0:T(8,128)(2,1)}) %all-gather.2.cloned.1.call-update) | async-done | bytes 2097168 | tf_op jit(solution)/shard_map/all_gather | solution.py:98
  102.3 15.7 %while.30 = (s32[]{:T(128)}, f32[128,1024]{1,0:T(8,128)}, f32[3,128,1024]{2,1,0:T(8,128)}, s32[]{:T(128)}, bf16[1024,1024]{1,0:T(8,128)(2,1)S(1)}, /*index=5*/f3...) while((s32[]{:T(128)}, f32[128,1024]{1,0:T(8,128)}, ...), condition=%wide.region_1.2_spmd, body=%wide.region_0.1_spmd.sunk | while | flops 2150760448 | bytes 25706640 | solution.py:114
  104.0 2.4 fusion.174
  106.4 3.2 fusion.175
  109.5 3.3 fusion.176
  113.7 3.6 fusion.177
  118.0 34.9 %collective-permute-start = (f32[128,1024]{1,0:T(8,128)}, f32[128,1024]{1,0:T(8,128)S(1)}, u32[]{:S(2)}, u32[]{:S(2)}) collective-permute-start(f32[128,1024]{1,0:T(8,128)} %get-tuple-element.170), channel_id=1, source_target_pairs={{0,32},{32,64},{64,96},{1,33},{33,65},{65,97},{2,34},{34,66},{66,9... | collective-permute-start | bytes 1572872 | tf_op jit(solution)/shard_map/ppermute | solution.py:23
  152.9 6.4 collective-permute-done
  160.4 1.9 collective-permute-start.1
  163.0 8.7 %collective-permute-done.1 = f32[128,1024]{1,0:T(8,128)} collective-permute-done((f32[128,1024]{1,0:T(8,128)S(1)}, f32[128,1024]{1,0:T(8,128)}, u32[]{:S(2)}, u32[]{:S(2)}) %collective-permute-start.1) | collective-permute-done | bytes 524320 | tf_op jit(solution)/shard_map/ppermute | solution.py:23
  173.1 2.5 broadcast.47.clone
  175.6 2.5 broadcast.47
  178.1 21.9 %while.31 = (s32[]{:T(128)}, f32[128,1024]{1,0:T(8,128)S(1)}, f32[1024,1024]{1,0:T(8,128)}, f32[1024,1024]{1,0:T(8,128)}, f32[1024]{0:T(1024)S(1)}, /*index=5*/s...) while((s32[]{:T(128)}, f32[128,1024]{1,0:T(8,128)S(1)}, ...), condition=%wide.region_7.8_spmd, body=%wide.region_2.7_spmd.sunk | while | flops 6195249152 | bytes 161800576 | solution.py:143
  197.4 2.0 copy-done.2
  200.0 5.0 broadcast_multiply_fusion.1
  205.1 5.0 broadcast_multiply_fusion
  212.0 80.2 %all-reduce = f32[1024]{0:T(1024)S(1)} all-reduce(f32[1024]{0:T(1024)S(1)} %broadcast_multiply_fusion.2), channel_id=4, replica_groups=mesh['seg'=4,'batch'=32] {'batch'}, use_global_device_ids=true, to_apply=%region_12.13.clone | all-reduce | flops 1024 | bytes 8192
  292.2 58.2 %psum.23 = f32[32]{0:T(128)} all-reduce(f32[32]{0:T(128)S(1)} %dynamic-slice.1), channel_id=1, replica_groups=mesh['seg'=4,'batch'=32] {'seg'}, use_global_device_ids=true, to_apply=%region_13.14 | all-reduce | flops 32 | bytes 256 | tf_op jit(solution)/shard_map/psum | solution.py:155
  350.4 62.5 %reduce-scatter.3.cloned.1.call-done = f32[32,1024]{1,0:T(8,128)} async-done(((f32[1024,1024]{1,0:T(8,128)}), f32[32,1024]{1,0:T(8,128)}) %reduce-scatter.3.cloned.1.call-update) | async-done | bytes 131088 | tf_op jit(solution)/shard_map/reduce_scatter | solution.py:151
  413.0 191.6 %reduce-scatter.5.cloned.1.call-done = f32[32,1024]{1,0:T(8,128)} async-done(((f32[1024,1024]{1,0:T(8,128)}), f32[32,1024]{1,0:T(8,128)}) %reduce-scatter.5.cloned.1.call-update) | async-done | bytes 131088 | tf_op jit(solution)/shard_map/reduce_scatter | solution.py:152
  605.5 56.1 %all-reduce.4.cloned.1.call-done = (f32[32,1024]{1,0:T(8,128)}, f32[32,1024]{1,0:T(8,128)}) async-done(((f32[32,1024]{1,0:T(8,128)}, f32[32,1024]{1,0:T(8,128)}), (f32[32,1024]{1,0:T(8,128)}, f32[32,1024]{1,0:T(8,128)})) %all-reduce.4.cloned.1.call-update) | async-done | bytes 262160 | tf_op jit(solution)/shard_map/psum | solution.py:155
  (62 shorter events, 30.9 us)
Async XLA Ops:
  7.2 93.8 %all-gather.2.cloned.1.call-start = ((), (), s32[]{:S(2)}) async-start(), calls=%async_computation.3 | async-start | bytes 2162688 | tf_op jit(solution)/shard_map/all_gather | solution.py:98
  10.3 11.4 %copy-start.7 = (f32[1,128,1024]{2,1,0:T(8,128)S(1)}, f32[1,128,1024]{2,1,0:T(8,128)}, u32[]{:S(2)}) copy-start(f32[1,128,1024]{2,1,0:T(8,128)} %param.10) | copy-start | bytes 1572868
  10.3 40.4 %all-to-all-start = ((bf16[32,32,1024]{2,1,0:T(8,128)(2,1)}), bf16[32,32,1024]{2,1,0:T(8,128)(2,1)S(1)}, u32[]{:S(2)}, u32[]{:S(2)}) async-start(bf16[32,32,1024]{2,1,0:T(8,128)(2,1)} %stack.86), calls=%async_computation | async-start | bytes 4194304 | tf_op jit(solution)/shard_map/all_to_all | solution.py:16
  21.6 80.7 %copy-start.6 = (f32[1024]{0:T(1024)S(1)}, f32[1024]{0:T(1024)}, u32[]{:S(2)}) copy-start(f32[1024]{0:T(1024)} %param.14) | copy-start | bytes 12292
  21.6 391.3 %reduce-scatter.3.cloned.1.call-start = ((), (), s32[]{:S(2)}) async-start(), calls=%async_computation.4 | async-start | bytes 4325376 | tf_op jit(solution)/shard_map/reduce_scatter | solution.py:151
  118.0 41.3 %collective-permute-start = (f32[128,1024]{1,0:T(8,128)}, f32[128,1024]{1,0:T(8,128)S(1)}, u32[]{:S(2)}, u32[]{:S(2)}) collective-permute-start(f32[128,1024]{1,0:T(8,128)} %get-tuple-element.170), channel_id=1, source_target_pairs={{0,32},{32,64},{64,96},{1,33},{33,65},{65,97},{2,34},{34,66},{66,9... | collective-permute-start | bytes 1572872 | tf_op jit(solution)/shard_map/ppermute | solution.py:23
  160.4 11.2 %collective-permute-start.1 = (f32[128,1024]{1,0:T(8,128)S(1)}, f32[128,1024]{1,0:T(8,128)}, u32[]{:S(2)}, u32[]{:S(2)}) collective-permute-start(f32[128,1024]{1,0:T(8,128)S(1)} %subtract_multiply_fusion), channel_id=1, source_target_pairs={{32,0},{64,32},{96,64},{33,1},{65,33},{97,65},{34,2},{66,34},{98,6... | collective-permute-start | bytes 1572872 | tf_op jit(solution)/shard_map/ppermute | solution.py:23
  179.0 2.8 copy-start
  179.0 2.8 copy-start.5
  191.1 2.2 copy-start.3
  193.2 2.2 copy-start.1
  195.4 2.0 copy-start.4
  197.4 2.0 copy-start.2
  205.0 399.6 %reduce-scatter.5.cloned.1.call-start = ((), (), s32[]{:S(2)}) async-start(), calls=%async_computation.5 | async-start | bytes 4325376 | tf_op jit(solution)/shard_map/reduce_scatter | solution.py:152
  210.1 0.7 copy-start.8
  210.1 451.5 %all-reduce.4.cloned.1.call-start = ((), (), s32[]{:S(2)}) async-start(), calls=%async_computation.6 | async-start | bytes 524288 | tf_op jit(solution)/shard_map/psum | solution.py:155
Sparse Core Ops, SparseCore 0:
  11.1 89.8 all-gather.1
  205.1 207.7 reduce-scatter.2
  415.4 189.2 reduce-scatter.4
  607.0 54.5 all-reduce.3
